TPU v7x, 32 devices: a whole 2x2x4 slice. The times are simulated.
32 devices in a mesh: dp: 16 (over z, y, core), tensor: 2 (over x).
Axes of the slice: x: 2, y: 2, z: 4, core: 2. Of those that a mesh axis runs over, the one named last changes fastest.
Arguments:
- block_input: bfloat16 [16384, 1536], P('dp'), may hold values from -50 to 50
- cotangent: bfloat16 [16384, 1536], P('dp'), may hold values from -6 to 6
- pre_gain: float32 [1536], replicated, may hold values from 0.5 to 1.5
- gate_proj: bfloat16 [1536, 3072], P(None, 'tensor'), may hold values from -0.15625 to 0.15625
- value_proj: bfloat16 [1536, 3072], P(None, 'tensor'), may hold values from -0.15625 to 0.15625
- step_proj: bfloat16 [1536, 48], P(None, 'tensor'), may hold values from -0.15625 to 0.15625
- state_proj: bfloat16 [1536, 256], replicated, may hold values from -0.15625 to 0.15625
- conv_value: float32 [4, 3072], P(None, 'tensor'), may hold values from -3 to 3
- conv_value_bias: float32 [3072], P('tensor'), may hold values from -3 to 3
- conv_state: float32 [4, 256], replicated, may hold values from -3 to 3
- conv_state_bias: float32 [256], replicated, may hold values from -3 to 3
- step_bias: float32 [48], P('tensor'), may hold values from -6.9 to -2.3
- decay_log: float32 [48], P('tensor'), may hold values from 0 to 2.77
- skip_gain: float32 [48], P('tensor'), may hold values from 0.5 to 1.5
- norm_gain: float32 [3072], P('tensor'), may hold values from 0.5 to 1.5
- out_proj: bfloat16 [3072, 1536], P('tensor'), may hold values from -0.109375 to 0.109375
Outputs:
- block_out: bfloat16 [16384, 1536], P('dp')
- grad_input: float32 [16384, 1536], P('dp')
- grad_pre_gain: float32 [1536], replicated
- grad_gate_proj: float32 [1536, 3072], P(None, 'tensor')
- grad_value_proj: float32 [1536, 3072], P(None, 'tensor')
- grad_step_proj: float32 [1536, 48], P(None, 'tensor')
- grad_state_proj: float32 [1536, 256], replicated
- grad_conv_value: float32 [4, 3072], P(None, 'tensor')
- grad_conv_value_bias: float32 [3072], P('tensor')
- grad_conv_state: float32 [4, 256], replicated
- grad_conv_state_bias: float32 [256], replicated
- grad_step_bias: float32 [48], P('tensor')
- grad_decay_log: float32 [48], P('tensor')
- grad_skip_gain: float32 [48], P('tensor')
- grad_norm_gain: float32 [3072], P('tensor')
- grad_out_proj: float32 [3072, 1536], P('tensor')
All inputs are finite; a program needn't handle non-finite values.
Results may differ from a plain program's by a relative error of at most 0.008.
Values may be sent and summed in bfloat16 or wider, within the bound.
No kernel may reach another device: no remote copies, remote signals or barrier semaphores. Data moves between devices by JAX's collectives and lax.ppermute only.
A program may use at most 256 MiB of HBM per device.

v0:
```python
import jax
import jax.numpy as jnp
from jax import lax
from jax.sharding import PartitionSpec as P

D = 1536
BLOCK = 256
SEQ_LEN = 1024
INNER = 3072
epsilon = 1e-05
highest = lax.Precision.HIGHEST


def causal_conv(values, kernel, offset):
    kernel_width = kernel.shape[0]
    length = values.shape[0]
    padded = jnp.concatenate(
        [jnp.zeros((kernel_width - 1, values.shape[1]), jnp.float32), values], axis=0
    )
    running_sum = jnp.zeros_like(values) + offset[None, :]
    for tap_index in range(kernel_width):
        running_sum = (
            running_sum + kernel[tap_index][None, :] * padded[tap_index : tap_index + length]
        )
    return running_sum


def make_states(bc_raw, conv_state, conv_state_bias):
    return jax.nn.silu(causal_conv(bc_raw, conv_state, conv_state_bias))


def mixer(
    conv_in,
    states,
    step_raw,
    gate_raw,
    conv_value,
    conv_value_bias,
    step_bias,
    decay_log,
    skip_gain,
):
    length = conv_in.shape[0]
    head_count = skip_gain.shape[0]
    head_width = conv_in.shape[1] // head_count
    state_width = states.shape[1] // 2
    block_count = length // BLOCK
    conv_out = jax.nn.silu(causal_conv(conv_in, conv_value, conv_value_bias))
    step_size = jax.nn.softplus(step_raw + step_bias[None, :])
    decay_rate = -jnp.exp(decay_log)
    log_decay = step_size * decay_rate[None, :]
    writer = states[:, :state_width].reshape(block_count, BLOCK, state_width)
    reader = states[:, state_width:].reshape(block_count, BLOCK, state_width)
    head_values = conv_out.reshape(block_count, BLOCK, head_count, head_width)
    cumulative = jnp.cumsum(log_decay.reshape(block_count, BLOCK, head_count), axis=1)
    cum_heads = jnp.transpose(cumulative, (0, 2, 1))
    step_heads = jnp.transpose(step_size.reshape(block_count, BLOCK, head_count), (0, 2, 1))
    scores = jnp.einsum("ktn,ksn->kts", reader, writer, precision=highest)
    causal_mask = jnp.tril(jnp.ones((BLOCK, BLOCK), jnp.float32))
    log_gap = cum_heads[:, :, :, None] - cum_heads[:, :, None, :]
    decay = jnp.exp(jnp.where(causal_mask > 0, log_gap, 0.0)) * causal_mask
    weights = scores[:, None, :, :] * decay * step_heads[:, :, None, :]
    intra_part = jnp.einsum("khts,kshp->kthp", weights, head_values, precision=highest)
    tail_weight = jnp.exp(cum_heads[:, :, -1:] - cum_heads) * step_heads
    block_state = jnp.einsum(
        "ksn,khs,kshp->khnp", writer, tail_weight, head_values, precision=highest
    )
    block_fade = jnp.exp(cum_heads[:, :, -1])

    def advance(carried, item):
        new_part, keep_factor = item
        return (carried * keep_factor[:, None, None] + new_part, carried)

    initial = jnp.zeros((head_count, state_width, head_width), jnp.float32)
    _, entering = lax.scan(advance, initial, (block_state, block_fade))
    inter_part = (
        jnp.einsum("ktn,khnp->kthp", reader, entering, precision=highest)
        * jnp.exp(cumulative)[:, :, :, None]
    )
    mixed_out = intra_part + inter_part + skip_gain[None, None, :, None] * head_values
    mixed_out = mixed_out.reshape(length, head_count * head_width)
    return mixed_out * jax.nn.silu(gate_raw)


def dot_plain(left, right):
    return jnp.dot(left, right, preferred_element_type=jnp.float32)


def dot_inner(left, right):
    return lax.dot_general(
        left, right, (((0,), (0,)), ((), ())), preferred_element_type=jnp.float32
    )


def dot_outer(left, right):
    return lax.dot_general(
        left, right, (((1,), (1,)), ((), ())), preferred_element_type=jnp.float32
    )


def local(
    block_input,
    cotangent,
    pre_gain,
    gate_proj,
    value_proj,
    step_proj,
    state_proj,
    conv_value,
    conv_value_bias,
    conv_state,
    conv_state_bias,
    step_bias,
    decay_log,
    skip_gain,
    norm_gain,
    out_proj,
):
    row_count = block_input.shape[0]
    seq_count = row_count // SEQ_LEN

    def by_sequence(array):
        return array.reshape(seq_count, SEQ_LEN, array.shape[1])

    def by_row(array):
        return array.reshape(row_count, array.shape[2])

    input_f32 = block_input.astype(jnp.float32)
    pre_scale = lax.rsqrt(jnp.mean(input_f32 * input_f32, axis=1, keepdims=True) + epsilon)
    normed = (input_f32 * pre_scale * pre_gain[None, :]).astype(jnp.bfloat16)
    gate_raw = dot_plain(normed, gate_proj)
    conv_in = dot_plain(normed, value_proj)
    step_raw = dot_plain(normed, step_proj)
    bc_raw = dot_plain(normed, state_proj)
    states, state_back = jax.vjp(
        jax.vmap(make_states, in_axes=(0, None, None)),
        by_sequence(bc_raw),
        conv_state,
        conv_state_bias,
    )
    gated_seq, mixer_back = jax.vjp(
        jax.vmap(mixer, in_axes=(0, 0, 0, 0, None, None, None, None, None)),
        by_sequence(conv_in),
        states,
        by_sequence(step_raw),
        by_sequence(gate_raw),
        conv_value,
        conv_value_bias,
        step_bias,
        decay_log,
        skip_gain,
    )
    gated = by_row(gated_seq)
    square_sum = lax.psum(jnp.sum(gated * gated, axis=1), "tensor")
    gate_scale = lax.rsqrt(square_sum[:, None] / INNER + epsilon)
    gated_normed = (gated * gate_scale * norm_gain[None, :]).astype(jnp.bfloat16)
    branch = lax.psum(dot_plain(gated_normed, out_proj).astype(jnp.bfloat16), "tensor").astype(
        jnp.float32
    )
    block_out = (input_f32 + branch).astype(jnp.bfloat16)
    d_gn = dot_outer(cotangent, out_proj)
    grad_out_proj = dot_inner(gated_normed, cotangent)
    grad_norm_gain = jnp.sum(d_gn * gated * gate_scale, axis=0)
    gate_dot = lax.psum(jnp.sum(d_gn * norm_gain[None, :] * gated, axis=1), "tensor")
    d_gated = (
        gate_scale * norm_gain[None, :] * d_gn - gated * gate_scale**3 * gate_dot[:, None] / INNER
    )
    (
        d_conv_in,
        d_states,
        d_step_raw,
        d_gate_raw,
        grad_conv_value,
        grad_conv_value_bias,
        grad_step_bias,
        grad_decay_log,
        grad_skip_gain,
    ) = mixer_back(by_sequence(d_gated))
    state_total = lax.psum(by_row(d_states), "tensor")
    d_bc_raw, grad_conv_state, grad_conv_state_bias = state_back(by_sequence(state_total))
    gate_bf = by_row(d_gate_raw).astype(jnp.bfloat16)
    value_bf = by_row(d_conv_in).astype(jnp.bfloat16)
    step_bf = by_row(d_step_raw).astype(jnp.bfloat16)
    state_bf = by_row(d_bc_raw).astype(jnp.bfloat16)
    head_terms = (
        dot_outer(gate_bf, gate_proj)
        + dot_outer(value_bf, value_proj)
        + dot_outer(step_bf, step_proj)
    )
    d_normed = lax.psum(head_terms, "tensor") + dot_outer(state_bf, state_proj)
    grad_pre_gain = jnp.sum(d_normed * input_f32 * pre_scale, axis=0)
    pre_dot = jnp.sum(d_normed * pre_gain[None, :] * input_f32, axis=1, keepdims=True)
    grad_input = (
        cotangent.astype(jnp.float32)
        + pre_scale * pre_gain[None, :] * d_normed
        - input_f32 * pre_scale**3 * pre_dot / D
    )
    grad_gate_proj = dot_inner(normed, gate_bf)
    grad_value_proj = dot_inner(normed, value_bf)
    grad_step_proj = dot_inner(normed, step_bf)
    grad_state_proj = dot_inner(normed, state_bf)
    (
        grad_pre_gain,
        grad_gate_proj,
        grad_value_proj,
        grad_step_proj,
        grad_state_proj,
        grad_conv_value,
        grad_conv_value_bias,
        grad_conv_state,
        grad_conv_state_bias,
        grad_step_bias,
        grad_decay_log,
        grad_skip_gain,
        grad_norm_gain,
        grad_out_proj,
    ) = lax.psum(
        (
            grad_pre_gain,
            grad_gate_proj,
            grad_value_proj,
            grad_step_proj,
            grad_state_proj,
            grad_conv_value,
            grad_conv_value_bias,
            grad_conv_state,
            grad_conv_state_bias,
            grad_step_bias,
            grad_decay_log,
            grad_skip_gain,
            grad_norm_gain,
            grad_out_proj,
        ),
        "dp",
    )
    return (
        block_out,
        grad_input,
        grad_pre_gain,
        grad_gate_proj,
        grad_value_proj,
        grad_step_proj,
        grad_state_proj,
        grad_conv_value,
        grad_conv_value_bias,
        grad_conv_state,
        grad_conv_state_bias,
        grad_step_bias,
        grad_decay_log,
        grad_skip_gain,
        grad_norm_gain,
        grad_out_proj,
    )


def solution(mesh):
    placed = (
        P("dp", None),
        P("dp", None),
        P(),
        P(None, "tensor"),
        P(None, "tensor"),
        P(None, "tensor"),
        P(),
        P(None, "tensor"),
        P("tensor"),
        P(),
        P(),
        P("tensor"),
        P("tensor"),
        P("tensor"),
        P("tensor"),
        P("tensor", None),
    )
    return jax.shard_map(
        local,
        mesh=mesh,
        in_specs=placed,
        out_specs=(
            P("dp", None),
            P("dp", None),
            P(),
            P(None, "tensor"),
            P(None, "tensor"),
            P(None, "tensor"),
            P(),
            P(None, "tensor"),
            P("tensor"),
            P(),
            P(),
            P("tensor"),
            P("tensor"),
            P("tensor"),
            P("tensor"),
            P("tensor", None),
        ),
        check_vma=False,
    )
```

profile of v0, /device:TPU:0, one launch (start us, length us, event | category | flops | bytes accessed | tf_op | source)
XLA Modules:
  0.0 1340.4 jit_solution(6802195912920558726)
XLA Ops:
  42.9 10.0 reshape.687
  71.3 10.3 fusion.83
  85.1 23.3 %while.34 = (s32[]{:T(128)}, f32[1,24,128,64]{3,2,1,0:T(8,128)S(1)}, f32[4,1,24,128,64]{4,3,2,1,0:T(8,128)}, f32[4,1,24,1,1]{2,4,3,1,0:T(1,128)S(1)}, f32[4,1,24...) while((s32[]{:T(128)}, f32[1,24,128,64]{3,2,1,0:T(8,128)S(1)}, ...), condition=%wide.region_4.5_spmd.clone, body=%wide.region_3.4_spmd.clone.sunk | while | flops 786435 | bytes 7865752 | solution.py:75
  124.4 9.8 copy.207
  134.3 33.3 %fusion.42 = f32[1,4,256,24,64]{2,4,3,1,0:T(8,128)} fusion(f32[1,4,256,24,64]{2,4,3,1,0:T(8,128)} %copy.207, f32[4,256,24,64]{1,3,2,0:T(8,128)} %bitcast.279, f32[24]{0:T(128)S(1)} %copy-done.93, f32[4,256,24]{1,2,0:T(8,128)S(1)} %bitcast.300, f32[4,24,256]{2,1,0:T(8,128)S(1)} %copy-done.48, f32[256,256]{1,0:T(8,128)S(1)} %copy-done.42, ...), kind=kOutput, calls=%fused_computation.68 | convolution fusion | flops 4869586944 | bytes 26837088 | tf_op jit(solution)/shard_map/jvp(vmap(khts,kshp->kthp))/dot_general | solution.py:63
  177.3 11.1 reshape.688
  188.4 12.5 multiply_reduce_fusion.10
  206.8 11.6 multiply_reduce_fusion.3
  223.3 11.5 fusion.28
  278.0 20.9 %fusion.89 = f32[4,256,128]{2,1,0:T(8,128)} fusion(f32[4,256,24,64]{1,0,3,2:T(4,128)S(1)} %copy-done.3, f32[4,256,24]{1,2,0:T(8,128)S(1)} %bitcast.301, f32[4,1,24,128,64]{4,3,2,1,0:T(8,128)S(1)} %bitcast.268), kind=kOutput, calls=%fused_computation.126 | convolution fusion | flops 2417491968 | bytes 10059776 | tf_op jit(solution)/shard_map/transpose(jvp(vmap(ktn,khnp->kthp)))/dot_general | solution.py:77
  299.0 45.9 %fusion.11 = (f32[4,24,256]{2,1,0:T(8,128)}, f32[4,24,256]{2,1,0:T(8,128)}, f32[4,24,256]{2,1,0:T(8,128)}, f32[4,256,256]{2,1,0:T(8,128)}) fusion(f32[4,24,256]{2,1,0:T(8,128)S(1)} %copy-done.49, f32[256,256]{1,0:T(8,128)S(1)} %copy-done.43, f32[4,24,256]{2,1,0:T(8,128)S(1)} %copy-done.52, f32[4,256,256]{2,1,0:T(8,128)S(1)} %copy-done.32, ...), kind=kOutput, calls=%fused_computation.30 | convolution fusion | flops 4925874176 | bytes 15499264 | tf_op jit(solution)/shard_map/transpose(jvp(vmap(khts,kshp->kthp)))/dot_general | solution.py:63
  356.0 26.0 %while.35 = (s32[]{:T(128)}, f32[1,24,128,64]{3,2,1,0:T(8,128)S(1)}, f32[4,1,24,128,64]{4,3,2,1,0:T(8,128)}, f32[4,1,24]{2,1,0:T(1,128)S(1)}, f32[4,1,24,128,64]...) while((s32[]{:T(128)}, ...), condition=%wide.region_12.13_spmd.clone, body=%wide.region_10.12_spmd.clone.sunk | while | flops 1179628 | bytes 8652312 | solution.py:75
  382.2 12.6 fusion.80
  397.5 27.4 %bitcast_add_fusion.2 = f32[1,4,256,24,64]{2,4,3,1,0:T(8,128)} fusion(f32[4,256,24,64]{1,3,2,0:T(8,128)S(1)} %fusion.80, f32[4,256,24,64]{1,0,3,2:T(4,128)} %reshape.659, f32[24]{0:T(128)S(1)} %copy-done.93, f32[4,256,24]{1,2,0:T(8,128)S(1)} %copy-done.35, f32[4,24,256]{2,1,0:T(8,128)S(1)} %copy-done.50, f32[256,256]{1,0:T(8,128)S(1)} %copy-done.44, ...), kind=kOutput, calls=%fused_computation.66 | convolution fusion | flops 4869586944 | bytes 26837088 | tf_op jit(solution)/shard_map/transpose(jvp(vmap(khts,kshp->kthp)))/dot_general | solution.py:63
  425.0 10.1 multiply_reduce_fusion.2
  445.9 10.0 reduce-window.16
  466.3 11.1 reshape.689
  477.5 14.4 %multiply_reduce_fusion.6 = (f32[1536]{0:T(1024)S(1)}, f32[1536]{0:T(1024)S(1)}, f32[1536]{0:T(1024)S(1)}, f32[1536]{0:T(1024)S(1)}, f32[1536]{0:T(1024)S(1)}, /*index=5*/f32[1,1024,1536]{2,1,0:T(8,128)S(1)}) fusion(f32[1,1024,1536]{2,1,0:T(8,128)} %bitcast.270, f32[1024,1536]{1,0:T(8,128)} %copy-done.2, f32[1,1024,1536]{2,1,0:T(8,128)} %get-tuple-element.386, ...), kind=kLoop, calls=%fused_computation.80 | loop fusion | flops 28303872 | bytes 31488000 | tf_op jit(solution)/shard_map/transpose(jvp(vmap()))/reduce_sum | solution.py:23
  527.5 9.9 convolution_convert_fusion
  540.6 10.4 fusion.145
  566.6 138.1 %all-reduce.33.cloned.1.call-done = (f32[1024,1536]{1,0:T(8,128)}, f32[1,1024,256]{2,1,0:T(8,128)}) async-done(((f32[1024,1536]{1,0:T(8,128)}, f32[1,1024,256]{2,1,0:T(8,128)}), (f32[1024,1536]{1,0:T(8,128)}, f32[1,1024,256]{2,1,0:T(8,128)})) %all-reduce.33.cloned.1.call-update) | async-done | bytes 7340048 | tf_op jit(solution)/shard_map/psum | solution.py:190
  719.2 62.5 %all-reduce.22 = (f32[1536]{0:T(1024)}, f32[4,1536]{1,0:T(4,128)}, f32[1536]{0:T(1024)}, f32[4,256]{1,0:T(4,128)}, f32[256]{0:T(256)}, /*index=5*/f32[24]{0:T(128)}, f32[24]{0:T(128)}, f32[24]{0:T(128)}, f32[1536]{0:T(1024)}) all-reduce(f32[1536]{0:T(1024)S(1)} %get-tuple-element.314, ...), channel_id=1, replica_groups=mesh['dp'=16,'tensor'=2] {'dp'}, use_global_device_ids=true, to_apply=%region_25.26 | all-reduce | flops 12104 | bytes 96832 | tf_op jit(solution)/shard_map/psum | solution.py:217
  781.6 11.2 all-reduce.29.cloned.1.call-done
  801.9 509.1 %all-reduce.31.cloned.1.call-done = (f32[1536,1536]{1,0:T(8,128)}, f32[1536,1536]{1,0:T(8,128)}, f32[1536,24]{0,1:T(8,128)}, f32[1536,256]{1,0:T(8,128)}, f32[1536,1536]{1,0:T(8,128)}) async-done(((f32[1536,1536]{1,0:T(8,128)}, f32[1536,1536]{1,0:T(8,128)}, f32[1536,24]{0,1:T(8,128)}, f32[1536,256]{1,0:T(8,128)}, f32[1536,1536]{1,0:T(8,128)}), (f32[1536,1536]{1,0:T(8,128)}, f32[1536,1536]{1,0:T(8,128)}, ...) | async-done | bytes 30031888 | tf_op jit(solution)/shard_map/psum | solution.py:217
  (391 shorter events, 320.5 us)
Async XLA Ops:
  7.2 48.8 %copy-start = (bf16[1536,256]{1,0:T(8,128)(2,1)S(1)}, bf16[1536,256]{1,0:T(8,128)(2,1)}, u32[]{:S(2)}) copy-start(bf16[1536,256]{1,0:T(8,128)(2,1)} %param.26) | copy-start | bytes 2359300
  7.2 697.5 %all-reduce.33.cloned.1.call-start = ((), (), s32[]{:S(2)}) async-start(), calls=%async_computation.2 | async-start | bytes 14680064 | tf_op jit(solution)/shard_map/psum | solution.py:190
  134.2 33.4 %copy-start.51 = (f32[4,24,256]{2,1,0:T(8,128)}, f32[4,24,256]{2,1,0:T(8,128)S(1)}, u32[]{:S(2)}) copy-start(f32[4,24,256]{2,1,0:T(8,128)S(1)} %reduce_window_sum.55) | copy-start | bytes 294916
  206.8 28.0 %copy-start.69 = (f32[1024]{0:T(1024)}, f32[1024]{0:T(1024)S(1)}, u32[]{:S(2)}) copy-start(f32[1024]{0:T(1024)S(1)} %get-tuple-element.408) | copy-start | bytes 12292
  270.3 28.6 %slice-start.2 = ((s8[6291456]{0:T(1024)(128)(4,1)}), s8[2097152]{0:T(1024)(128)(4,1)S(1)}, s32[]{:S(2)}) async-start(s8[6291456]{0:T(1024)(128)(4,1)} %bitcast.271), calls=%async_computation.5 | async-start | bytes 4194304
  277.9 21.0 %copy-start.18 = (f32[1,4,256,24,64]{2,1,4,3,0:T(4,128)S(1)}, f32[1,4,256,24,64]{2,1,4,3,0:T(4,128)}, u32[]{:S(2)}) copy-start(f32[1,4,256,24,64]{2,1,4,3,0:T(4,128)} %reshape.662) | copy-start | bytes 18874372
  277.9 21.0 %copy-start.32 = (f32[4,256,256]{2,1,0:T(8,128)S(1)}, f32[4,256,256]{2,1,0:T(8,128)}, u32[]{:S(2)}) copy-start(f32[4,256,256]{2,1,0:T(8,128)} %copy-done.31) | copy-start | bytes 3145732
  277.9 21.0 %copy-start.43 = (f32[256,256]{1,0:T(8,128)S(1)}, f32[256,256]{1,0:T(8,128)}, u32[]{:S(2)}) copy-start(f32[256,256]{1,0:T(8,128)} %fusion.108) | copy-start | bytes 786436
  277.9 21.0 %copy-start.49 = (f32[4,24,256]{2,1,0:T(8,128)S(1)}, f32[4,24,256]{2,1,0:T(8,128)}, u32[]{:S(2)}) copy-start(f32[4,24,256]{2,1,0:T(8,128)} %get-tuple-element.418) | copy-start | bytes 294916
  277.9 21.0 %copy-start.52 = (f32[4,24,256]{2,1,0:T(8,128)S(1)}, f32[4,24,256]{2,1,0:T(8,128)}, u32[]{:S(2)}) copy-start(f32[4,24,256]{2,1,0:T(8,128)} %copy-done.51) | copy-start | bytes 294916
  277.9 21.0 %copy-start.65 = (pred[256,256]{1,0:T(8,128)(4,1)S(1)}, pred[256,256]{1,0:T(8,128)(4,1)}, u32[]{:S(2)}) copy-start(pred[256,256]{1,0:T(8,128)(4,1)} %broadcast_compare_fusion) | copy-start | bytes 196612
  382.1 42.8 %slice-start.4 = ((s8[6291456]{0:T(1024)(128)(4,1)}), s8[4194304]{0:T(1024)(128)(4,1)S(1)}, s32[]{:S(2)}) async-start(s8[6291456]{0:T(1024)(128)(4,1)} %bitcast.273), calls=%async_computation.7 | async-start | bytes 8388608
  382.2 55.2 %slice-start.6 = ((s8[6291456]{0:T(1024)(128)(4,1)}), s8[4194304]{0:T(1024)(128)(4,1)S(1)}, s32[]{:S(2)}) async-start(s8[6291456]{0:T(1024)(128)(4,1)} %bitcast.275), calls=%async_computation.9 | async-start | bytes 8388608
  397.5 27.5 %slice-start.5 = ((s8[6291456]{0:T(1024)(128)(4,1)}), s8[2097152]{0:T(1024)(128)(4,1)S(1)}, s32[]{:S(2)}) async-start(s8[6291456]{0:T(1024)(128)(4,1)} %bitcast.273), calls=%async_computation.8 | async-start | bytes 4194304
  397.5 39.9 %slice-start.7 = ((s8[6291456]{0:T(1024)(128)(4,1)}), s8[2097152]{0:T(1024)(128)(4,1)S(1)}, s32[]{:S(2)}) async-start(s8[6291456]{0:T(1024)(128)(4,1)} %bitcast.275), calls=%async_computation.10 | async-start | bytes 4194304
  526.8 266.0 %all-reduce.29.cloned.1.call-start = ((), (), s32[]{:S(2)}) async-start(), calls=%async_computation | async-start | bytes 6291456 | tf_op jit(solution)/shard_map/psum | solution.py:157
  537.5 773.5 %all-reduce.31.cloned.1.call-start = ((), (), s32[]{:S(2)}) async-start(), calls=%async_computation.1 | async-start | bytes 60063744 | tf_op jit(solution)/shard_map/psum | solution.py:217
  558.6 146.0 %copy-start.12 = (f32[1024,256]{1,0:T(8,128)S(1)}, f32[1024,256]{1,0:T(8,128)}, u32[]{:S(2)}) copy-start(f32[1024,256]{1,0:T(8,128)} %copy-done.11) | copy-start | bytes 3145732
  558.7 146.0 %copy-start.19 = (f32[1,1024,256]{2,1,0:T(8,128)S(1)}, f32[1,1024,256]{2,1,0:T(8,128)}, u32[]{:S(2)}) copy-start(f32[1,1024,256]{2,1,0:T(8,128)} %get-tuple-element.384) | copy-start | bytes 3145732
  558.7 148.1 %copy-start.79 = (f32[1,256]{1,0:T(1,128)S(1)}, f32[1,256]{1,0:T(1,128)}, u32[]{:S(2)}) copy-start(f32[1,256]{1,0:T(1,128)} %copy-done.78) | copy-start | bytes 3076
  558.7 148.1 %copy-start.81 = (f32[1,256]{1,0:T(1,128)S(1)}, f32[1,256]{1,0:T(1,128)}, u32[]{:S(2)}) copy-start(f32[1,256]{1,0:T(1,128)} %copy-done.80) | copy-start | bytes 3076
  558.7 148.1 %copy-start.83 = (f32[1,256]{1,0:T(1,128)S(1)}, f32[1,256]{1,0:T(1,128)}, u32[]{:S(2)}) copy-start(f32[1,256]{1,0:T(1,128)} %copy-done.82) | copy-start | bytes 3076
  558.7 148.1 %copy-start.85 = (f32[1,256]{1,0:T(1,128)S(1)}, f32[1,256]{1,0:T(1,128)}, u32[]{:S(2)}) copy-start(f32[1,256]{1,0:T(1,128)} %copy-done.84) | copy-start | bytes 3076
  711.9 81.0 %copy-start.77 = (f32[1024]{0:T(1024)S(1)}, f32[1024]{0:T(1024)}, u32[]{:S(2)}) copy-start(f32[1024]{0:T(1024)} %get-tuple-element.405) | copy-start | bytes 12292
  (89 other events, 829.2 us)
Sparse Core Ops, SparseCore 0:
  526.9 177.7 all-reduce.32
  707.0 85.8 all-reduce.28
  799.3 511.6 all-reduce.30
where the time goes:
time: 1350 us; the launch traced here: 1340 us
  waiting for transfers between devices  658 us (49%)
  matrix products  283 us (21%)
  local copies, waits for them, and re-layouts  176 us (13%)
  other arithmetic  134 us (10%)
  blocking collectives  73.2 us (5%)
  between operations  15.7 us (1%)
    psum x1, waiting for transfers between devices, local(): lax.psum((grad_pre_gain, grad_gate_proj, grad_value_proj, grad_step_proj,...  509 us
    psum x1, waiting for transfers between devices, local(): d_normed = lax.psum(head_terms, 'tensor') + dot_outer(state_bf, state_proj)  138 us
    dot_general x3, matrix products, mixer(): jnp.einsum('khts,kshp->kthp', weights, head_values, precision=highest)  107 us
    psum x1, blocking collectives, local(): lax.psum((grad_pre_gain, grad_gate_proj, grad_value_proj, grad_step_proj,...  62.5 us
    reshape x4, local copies, waits for them, and re-layouts, mixer(): head_values = conv_out.reshape(block_count, BLOCK, head_count, head_width)  40.7 us
    dot_general x5, matrix products, dot_outer(): lax.dot_general(left, right, (((1,), (1,)), ((), ())), preferred_element_...  40 us
    reshape x4, local copies, waits for them, and re-layouts, mixer(): mixed_out = mixed_out.reshape(length, head_count * head_width)  37.4 us
    unnamed x228, local copies, waits for them, and re-layouts  34.9 us
  transfers between devices with their start and end apart: 3, of which 3 were waited for; matrix products, arithmetic and copies ran while one was open for 5% of the time, Pallas kernels for 0%

commit v1 on v0

--- a/solution.py
+++ b/solution.py
@@ -1,3 +1,4 @@
+import functools
 import jax
 import jax.numpy as jnp
 from jax import lax
@@ -9,6 +10,14 @@
 INNER = 3072
 epsilon = 1e-05
 highest = lax.Precision.HIGHEST
+
+
+def take_bands(inputs, across):
+    out_arr = jnp.sum(lax.all_gather(inputs, axis_name=across), 0)
+    return out_arr
+
+
+tails_render = functools.partial(take_bands, across="tensor")
 
 
 def causal_conv(values, kernel, offset):
@@ -187,7 +196,7 @@
         + dot_outer(value_bf, value_proj)
         + dot_outer(step_bf, step_proj)
     )
-    d_normed = lax.psum(head_terms, "tensor") + dot_outer(state_bf, state_proj)
+    d_normed = tails_render(head_terms) + dot_outer(state_bf, state_proj)
     grad_pre_gain = jnp.sum(d_normed * input_f32 * pre_scale, axis=0)
     pre_dot = jnp.sum(d_normed * pre_gain[None, :] * input_f32, axis=1, keepdims=True)
     grad_input = (

time: 1350 us -> 1330 us (0.985)
  waiting for transfers between devices: 658 us -> 625 us
    psum x1, waiting for transfers between devices: 138 us -> 0.02 us  [local(): state_total = lax.psum(by_row(d_states), 'tensor')]
    all_gather x0 -> x1, waiting for transfers between devices: none -> 106 us  [take_bands(): out_arr = jnp.sum(lax.all_gather(inputs, axis_name=across), 0)]
    unnamed x228 -> x210, local copies, waits for them, and re-layouts: 34.9 us -> 28.1 us
  transfers between devices with their start and end apart: 3 -> 4, of which waited for: 3 -> 3; matrix products, arithmetic and copies ran while one was open for 5% -> 16% of each run, Pallas kernels for 0% -> 0%
where the time goes in v1:
time: 1330 us; the launch traced here: 1320 us
  waiting for transfers between devices  625 us (47%)
  matrix products  295 us (22%)
  local copies, waits for them, and re-layouts  169 us (13%)
  other arithmetic  144 us (11%)
  blocking collectives  72.5 us (5%)
  between operations  15.4 us (1%)
    psum x1, waiting for transfers between devices, local(): lax.psum((grad_pre_gain, grad_gate_proj, grad_value_proj, grad_step_proj,...  509 us
    all_gather x1, waiting for transfers between devices, take_bands(): out_arr = jnp.sum(lax.all_gather(inputs, axis_name=across), 0)  106 us
    dot_general x3, matrix products, mixer(): jnp.einsum('khts,kshp->kthp', weights, head_values, precision=highest)  105 us
    psum x1, blocking collectives, local(): lax.psum((grad_pre_gain, grad_gate_proj, grad_value_proj, grad_step_proj,...  61.8 us
    reshape x4, local copies, waits for them, and re-layouts, mixer(): head_values = conv_out.reshape(block_count, BLOCK, head_count, head_width)  40.8 us
    dot_general x5, matrix products, dot_outer(): lax.dot_general(left, right, (((1,), (1,)), ((), ())), preferred_element_...  39.4 us
    dot_general x3, matrix products, mixer(): jnp.einsum('ksn,khs,kshp->khnp', writer, tail_weight, head_values, precis...  38.1 us
    reshape x4, local copies, waits for them, and re-layouts, mixer(): mixed_out = mixed_out.reshape(length, head_count * head_width)  37.3 us
  transfers between devices with their start and end apart: 4, of which 3 were waited for; matrix products, arithmetic and copies ran while one was open for 16% of the time, Pallas kernels for 0%

profile of v1, /device:TPU:0, one launch (start us, length us, event | category | flops | bytes accessed | tf_op | source)
XLA Modules:
  0.0 1320.9 jit_solution(5161816531156524545)
XLA Ops:
  42.9 10.0 reshape.688
  71.4 10.3 fusion.83
  85.2 23.4 %while.34 = (s32[]{:T(128)}, f32[1,24,128,64]{3,2,1,0:T(8,128)S(1)}, f32[4,1,24,128,64]{4,3,2,1,0:T(8,128)}, f32[4,1,24,1,1]{2,4,3,1,0:T(1,128)S(1)}, f32[4,1,24...) while((s32[]{:T(128)}, f32[1,24,128,64]{3,2,1,0:T(8,128)S(1)}, ...), condition=%wide.region_4.5_spmd.clone, body=%wide.region_3.4_spmd.clone.sunk | while | flops 786435 | bytes 7865752 | solution.py:84
  134.5 33.1 %fusion.42 = f32[1,4,256,24,64]{2,4,3,1,0:T(8,128)} fusion(f32[1,4,256,24,64]{2,4,3,1,0:T(8,128)} %copy.207, f32[4,256,24,64]{1,3,2,0:T(8,128)} %bitcast.280, f32[24]{0:T(128)S(1)} %copy-done.84, f32[4,256,24]{1,2,0:T(8,128)S(1)} %bitcast.302, f32[4,24,256]{2,1,0:T(8,128)S(1)} %copy-done.42, f32[256,256]{1,0:T(8,128)S(1)} %copy-done.36, ...), kind=kOutput, calls=%fused_computation.68 | convolution fusion | flops 4869586944 | bytes 26837088 | tf_op jit(solution)/shard_map/jvp(vmap(khts,kshp->kthp))/dot_general | solution.py:72
  177.4 11.1 reshape.689
  188.5 12.4 multiply_reduce_fusion.10
  206.8 11.7 multiply_reduce_fusion.3
  223.4 14.0 %fusion.43 = (f32[1536]{0:T(1024)}, f32[1024,1536]{1,0:T(8,128)}) fusion(f32[1,1024,1536]{2,1,0:T(8,128)} %get-tuple-element.384, f32[1024,1536]{1,0:T(8,128)} %get-tuple-element.412, f32[1024]{0:T(1024)S(1)} %psum.128, f32[1024,1536]{1,0:T(8,128)} %get-tuple-element.378, f32[1024]{0:T(1024)S(1)} %get-tuple-element.405, f32[1024,1536]{1,0:T(8,128)} %get-tuple-element.413, ...), kind=kLoop, calls=%fused_computation.70 | loop fusion | flops 26737152 | bytes 31481856 | tf_op jit(solution)/shard_map/transpose(jvp(vmap()))/reduce_sum | solution.py:89
  260.4 22.8 %fusion.89 = f32[4,256,128]{2,1,0:T(8,128)S(1)} fusion(f32[4,256,24,64]{1,0,3,2:T(4,128)} %reshape.659, f32[4,256,24]{1,2,0:T(8,128)S(1)} %bitcast.303, f32[4,1,24,128,64]{4,3,2,1,0:T(8,128)} %get-tuple-element.534), kind=kOutput, calls=%fused_computation.126 | convolution fusion | flops 2417491968 | bytes 10059776 | tf_op jit(solution)/shard_map/transpose(jvp(vmap(ktn,khnp->kthp)))/dot_general | solution.py:86
  283.3 45.0 %fusion.11 = (f32[4,24,256]{2,1,0:T(8,128)}, f32[4,24,256]{2,1,0:T(8,128)}, f32[4,24,256]{2,1,0:T(8,128)}, f32[4,256,256]{2,1,0:T(8,128)S(1)}) fusion(f32[4,24,256]{2,1,0:T(8,128)S(1)} %copy-done.43, f32[256,256]{1,0:T(8,128)S(1)} %copy-done.37, f32[4,24,256]{2,1,0:T(8,128)S(1)} %copy-done.46, f32[4,256,256]{2,1,0:T(8,128)S(1)} %copy-done.27, ...), kind=kOutput, calls=%fused_computation.30 | convolution fusion | flops 4925874176 | bytes 15499264 | tf_op jit(solution)/shard_map/transpose(jvp(vmap(khts,kshp->kthp)))/dot_general | solution.py:72
  343.2 25.9 %while.35 = (s32[]{:T(128)}, f32[1,24,128,64]{3,2,1,0:T(8,128)S(1)}, f32[4,1,24,128,64]{4,3,2,1,0:T(8,128)}, f32[4,1,24]{2,1,0:T(1,128)S(1)}, f32[4,1,24,128,64]...) while((s32[]{:T(128)}, ...), condition=%wide.region_12.13_spmd.clone, body=%wide.region_10.12_spmd.clone.sunk | while | flops 1179628 | bytes 8652312 | solution.py:84
  369.2 15.3 %fusion.97 = f32[1,4,256,128]{2,3,1,0:T(8,128)S(1)} fusion(f32[1,4,256,128]{2,3,1,0:T(8,128)} %convolution_bitcast_fusion, f32[4,256,24,64]{1,0,3,2:T(4,128)} %reshape.642, f32[4,256,24]{1,2,0:T(8,128)S(1)} %copy-done.30, f32[4,1,24,128,64]{4,3,2,1,0:T(8,128)} %get-tuple-element.193), kind=kOutput, calls=%fused_computation.128 | convolution fusion | flops 2417623040 | bytes 10584064 | tf_op jit(solution)/shard_map/transpose(jvp(vmap(ksn,khs,kshp->khnp)))/dot_general | solution.py:74
  385.8 12.6 fusion.28
  403.6 12.6 fusion.80
  416.2 27.0 %bitcast_add_fusion.2 = f32[1,4,256,24,64]{2,4,3,1,0:T(8,128)} fusion(f32[4,256,24,64]{1,3,2,0:T(8,128)S(1)} %fusion.80, f32[4,256,24,64]{1,0,3,2:T(4,128)S(1)} %bitcast.277, f32[24]{0:T(128)S(1)} %copy-done.84, f32[4,256,24]{1,2,0:T(8,128)S(1)} %copy-done.30, f32[4,24,256]{2,1,0:T(8,128)S(1)} %copy-done.44, f32[256,256]{1,0:T(8,128)S(1)} %copy-done.38, ...), kind=kOutput, calls=%fused_computation.66 | convolution fusion | flops 4869586944 | bytes 26837088 | tf_op jit(solution)/shard_map/transpose(jvp(vmap(khts,kshp->kthp)))/dot_general | solution.py:72
  451.0 10.0 reduce-window.16
  471.1 11.1 reshape.690
  482.2 14.6 %multiply_reduce_fusion.6 = (f32[1536]{0:T(1024)S(1)}, f32[1536]{0:T(1024)S(1)}, f32[1536]{0:T(1024)S(1)}, f32[1536]{0:T(1024)S(1)}, f32[1536]{0:T(1024)S(1)}, /*index=5*/f32[1,1024,1536]{2,1,0:T(8,128)S(1)}) fusion(f32[1,1024,1536]{2,1,0:T(8,128)} %bitcast.269, f32[1024,1536]{1,0:T(8,128)} %copy-done.2, f32[1,1024,1536]{2,1,0:T(8,128)} %get-tuple-element.384, ...), kind=kLoop, calls=%fused_computation.80 | loop fusion | flops 28303872 | bytes 31488000 | tf_op jit(solution)/shard_map/transpose(jvp(vmap()))/reduce_sum | solution.py:32
  531.3 10.0 convolution_convert_fusion
  545.3 11.5 fusion.145
  579.7 105.9 %all-gather.3.cloned.1.call-done = f32[2048,1536]{1,0:T(8,128)} async-done(((f32[1024,1536]{1,0:T(8,128)}), f32[2048,1536]{1,0:T(8,128)}) %all-gather.3.cloned.1.call-update) | async-done | bytes 12582928 | tf_op jit(solution)/shard_map/all_gather | solution.py:16
  701.9 61.8 %all-reduce.22 = (f32[1536]{0:T(1024)}, f32[4,1536]{1,0:T(4,128)}, f32[1536]{0:T(1024)}, f32[4,256]{1,0:T(4,128)}, f32[256]{0:T(256)}, /*index=5*/f32[24]{0:T(128)}, f32[24]{0:T(128)}, f32[24]{0:T(128)}, f32[1536]{0:T(1024)}) all-reduce(f32[1536]{0:T(1024)S(1)} %get-tuple-element.314, ...), channel_id=1, replica_groups=mesh['dp'=16,'tensor'=2] {'dp'}, use_global_device_ids=true, to_apply=%region_25.26 | all-reduce | flops 12104 | bytes 96832 | tf_op jit(solution)/shard_map/psum | solution.py:226
  763.7 10.1 all-reduce.28.cloned.1.call-done
  782.8 508.9 %all-reduce.32.cloned.1.call-done = (f32[1536,1536]{1,0:T(8,128)}, f32[1536,1536]{1,0:T(8,128)}, f32[1536,24]{0,1:T(8,128)}, f32[1536,256]{1,0:T(8,128)}, f32[1536,1536]{1,0:T(8,128)}) async-done(((f32[1536,1536]{1,0:T(8,128)}, f32[1536,1536]{1,0:T(8,128)}, f32[1536,24]{0,1:T(8,128)}, f32[1536,256]{1,0:T(8,128)}, f32[1536,1536]{1,0:T(8,128)}), (f32[1536,1536]{1,0:T(8,128)}, f32[1536,1536]{1,0:T(8,128)}, ...) | async-done | bytes 30031888 | tf_op jit(solution)/shard_map/psum | solution.py:226
  (377 shorter events, 323.6 us)
Async XLA Ops:
  7.2 48.9 %copy-start = (bf16[1536,256]{1,0:T(8,128)(2,1)S(1)}, bf16[1536,256]{1,0:T(8,128)(2,1)}, u32[]{:S(2)}) copy-start(bf16[1536,256]{1,0:T(8,128)(2,1)} %param.26) | copy-start | bytes 2359300
  7.2 565.3 %all-reduce.30.cloned.1.call-start = ((), (), s32[]{:S(2)}) async-start(), calls=%async_computation.1 | async-start | bytes 2097152 | tf_op jit(solution)/shard_map/psum | solution.py:188
  134.5 33.1 %copy-start.45 = (f32[4,24,256]{2,1,0:T(8,128)}, f32[4,24,256]{2,1,0:T(8,128)S(1)}, u32[]{:S(2)}) copy-start(f32[4,24,256]{2,1,0:T(8,128)S(1)} %reduce_window_sum.55) | copy-start | bytes 294916
  252.1 31.2 %slice-start = ((s8[6291456]{0:T(1024)(128)(4,1)}), s8[2097152]{0:T(1024)(128)(4,1)S(1)}, s32[]{:S(2)}) async-start(s8[6291456]{0:T(1024)(128)(4,1)} %bitcast.270), calls=%async_computation.4 | async-start | bytes 4194304
  260.3 22.9 %slice-start.1 = ((s8[6291456]{0:T(1024)(128)(4,1)}), s8[4194304]{0:T(1024)(128)(4,1)S(1)}, s32[]{:S(2)}) async-start(s8[6291456]{0:T(1024)(128)(4,1)} %bitcast.270), calls=%async_computation.5 | async-start | bytes 8388608
  260.3 22.9 %copy-start.14 = (f32[1,4,256,24,64]{2,1,4,3,0:T(4,128)S(1)}, f32[1,4,256,24,64]{2,1,4,3,0:T(4,128)}, u32[]{:S(2)}) copy-start(f32[1,4,256,24,64]{2,1,4,3,0:T(4,128)} %reshape.662) | copy-start | bytes 18874372
  260.3 22.9 %copy-start.27 = (f32[4,256,256]{2,1,0:T(8,128)S(1)}, f32[4,256,256]{2,1,0:T(8,128)}, u32[]{:S(2)}) copy-start(f32[4,256,256]{2,1,0:T(8,128)} %copy-done.26) | copy-start | bytes 3145732
  260.3 22.9 %copy-start.37 = (f32[256,256]{1,0:T(8,128)S(1)}, f32[256,256]{1,0:T(8,128)}, u32[]{:S(2)}) copy-start(f32[256,256]{1,0:T(8,128)} %fusion.108) | copy-start | bytes 786436
  260.3 22.9 %copy-start.43 = (f32[4,24,256]{2,1,0:T(8,128)S(1)}, f32[4,24,256]{2,1,0:T(8,128)}, u32[]{:S(2)}) copy-start(f32[4,24,256]{2,1,0:T(8,128)} %get-tuple-element.416) | copy-start | bytes 294916
  260.4 22.9 %copy-start.46 = (f32[4,24,256]{2,1,0:T(8,128)S(1)}, f32[4,24,256]{2,1,0:T(8,128)}, u32[]{:S(2)}) copy-start(f32[4,24,256]{2,1,0:T(8,128)} %copy-done.45) | copy-start | bytes 294916
  260.4 22.9 %copy-start.59 = (pred[256,256]{1,0:T(8,128)(4,1)S(1)}, pred[256,256]{1,0:T(8,128)(4,1)}, u32[]{:S(2)}) copy-start(pred[256,256]{1,0:T(8,128)(4,1)} %broadcast_compare_fusion) | copy-start | bytes 196612
  283.2 48.9 %slice-start.4 = ((s8[6291456]{0:T(1024)(128)(4,1)}), s8[4194304]{0:T(1024)(128)(4,1)S(1)}, s32[]{:S(2)}) async-start(s8[6291456]{0:T(1024)(128)(4,1)} %bitcast.274), calls=%async_computation.8 | async-start | bytes 8388608
  283.3 45.0 %copy-start.13 = (f32[1,1024,128]{2,1,0:T(8,128)S(1)}, f32[1,1024,128]{2,1,0:T(8,128)}, u32[]{:S(2)}) copy-start(f32[1,1024,128]{2,1,0:T(8,128)} %get-tuple-element.398) | copy-start | bytes 1572868
  283.3 48.8 %slice-start.5 = ((s8[6291456]{0:T(1024)(128)(4,1)}), s8[2097152]{0:T(1024)(128)(4,1)S(1)}, s32[]{:S(2)}) async-start(s8[6291456]{0:T(1024)(128)(4,1)} %bitcast.274), calls=%async_computation.9 | async-start | bytes 4194304
  343.2 26.0 %copy-start.30 = (f32[4,256,24]{1,2,0:T(8,128)S(1)}, f32[4,256,24]{1,2,0:T(8,128)}, u32[]{:S(2)}) copy-start(f32[4,256,24]{1,2,0:T(8,128)} %copy-done.29) | copy-start | bytes 294916
  385.8 299.9 %all-gather.3.cloned.1.call-start = ((), (), s32[]{:S(2)}) async-start(), calls=%async_computation.2 | async-start | bytes 18874368 | tf_op jit(solution)/shard_map/all_gather | solution.py:16
  403.5 39.7 %slice-start.2 = ((s8[6291456]{0:T(1024)(128)(4,1)}), s8[4194304]{0:T(1024)(128)(4,1)S(1)}, s32[]{:S(2)}) async-start(s8[6291456]{0:T(1024)(128)(4,1)} %bitcast.272), calls=%async_computation.6 | async-start | bytes 8388608
  416.2 27.0 %slice-start.3 = ((s8[6291456]{0:T(1024)(128)(4,1)}), s8[2097152]{0:T(1024)(128)(4,1)S(1)}, s32[]{:S(2)}) async-start(s8[6291456]{0:T(1024)(128)(4,1)} %bitcast.272), calls=%async_computation.7 | async-start | bytes 4194304
  531.2 242.6 %all-reduce.28.cloned.1.call-start = ((), (), s32[]{:S(2)}) async-start(), calls=%async_computation | async-start | bytes 6291456 | tf_op jit(solution)/shard_map/psum | solution.py:166
  541.2 750.5 %all-reduce.32.cloned.1.call-start = ((), (), s32[]{:S(2)}) async-start(), calls=%async_computation.3 | async-start | bytes 60063744 | tf_op jit(solution)/shard_map/psum | solution.py:226
  545.3 19.1 %slice-start.8 = ((s8[6291456]{0:T(1024)(128)(4,1)}), s8[4194304]{0:T(1024)(128)(4,1)S(1)}, s32[]{:S(2)}) async-start(s8[6291456]{0:T(1024)(128)(4,1)} %bitcast.278), calls=%async_computation.12 | async-start | bytes 8388608
  695.3 78.5 %copy-start.68 = (f32[1024]{0:T(1024)S(1)}, f32[1024]{0:T(1024)}, u32[]{:S(2)}) copy-start(f32[1024]{0:T(1024)} %get-tuple-element.403) | copy-start | bytes 12292
  1291.7 18.7 %slice-start.10 = ((s8[9437184]{0:T(1024)(128)(4,1)}), s8[4194304]{0:T(1024)(128)(4,1)S(1)}, s32[]{:S(2)}) async-start(s8[9437184]{0:T(1024)(128)(4,1)} %bitcast.294), calls=%async_computation.14 | async-start | bytes 8388608
  1291.7 18.7 %slice-start.11 = ((s8[9437184]{0:T(1024)(128)(4,1)}), s8[4194304]{0:T(1024)(128)(4,1)S(1)}, s32[]{:S(2)}) async-start(s8[9437184]{0:T(1024)(128)(4,1)} %bitcast.294), calls=%async_computation.15 | async-start | bytes 8388608
  (81 other events, 726.9 us)
Sparse Core Ops, SparseCore 0:
  385.9 41.8 all-reduce.29
  531.3 154.2 all-gather.2
  687.9 85.8 all-reduce.27
  780.1 511.6 all-reduce.31
